TPU v7x, 256 devices: a whole 4x4x8 slice. The times are simulated.
256 devices in a mesh: docs: 64 (over x, z, core), terms: 4 (over y).
Axes of the slice: x: 4, y: 4, z: 8, core: 2. Of those that a mesh axis runs over, the one named last changes fastest.
Arguments:
- values: bfloat16 [256, 64, 64, 128], P('docs', 'terms')
- block_ids: int32 [256, 64], P('docs', 'terms'), may hold values from 0 to 2047, as said below
- assignment: int32 [16384, 1], P('docs'), may hold values from 0 to 511
Outputs:
- coefficients: float32 [16384, 512], P('docs', 'terms')
Inputs may be any that keep to these rules, and one draw needn't show every extreme that they name: `assignment`: every one of the 512 clusters has at least one document. `block_ids`: in each term slice, the 16 blocks of one tile lie in 16 different ranges of 32 consecutive block numbers, and the tiles of one index of docs place exactly 1 block in each such range.
All inputs are finite; a program needn't handle non-finite values.
Results may differ from a plain program's by a relative error of at most 0.00045.
Values may be sent and summed in bfloat16 or wider, within the bound.
A program may use at most 128 MiB of HBM per device.

v0:
```python
import jax
import jax.numpy as jnp
from jax import lax
from jax.sharding import PartitionSpec as P

K = 512
BLK_OWN = 32
EPSILON = 1e-06
RIDGE_WEIGHT = 1.0


def send_order(owner, capacity):
    pairs = owner.shape[0]
    counter = jnp.arange(pairs, dtype=jnp.int32)
    same = owner[:, None] == owner[None, :]
    earlier = counter[None, :] < counter[:, None]
    rank = jnp.sum((same & earlier).astype(jnp.int32), axis=1)
    target = owner * capacity + rank
    source = jnp.zeros((pairs,), jnp.int32).at[target].set(counter)
    return (target, source)


def pick_tile(labels, tile_index):
    return labels[tile_index]


def body(values, block_ids, assignment):
    tiles_here, slot_count, tile_rows, block_width = values.shape
    peers = lax.axis_size("docs")
    pairs = tiles_here * slot_count
    capacity = pairs // peers
    arrivals = peers * capacity
    doc_rows = tiles_here * tile_rows
    all_blocks, all_labels = (
        lax.all_gather(block_ids, "docs", axis=0, tiled=True),
        lax.all_gather(assignment, "docs", axis=0, tiled=True),
    )
    own_target, own_source = send_order((block_ids // BLK_OWN).reshape(pairs), capacity)
    flat_values = values.reshape(pairs, tile_rows, block_width)
    outgoing = flat_values[own_source].reshape(peers, capacity, tile_rows, block_width)
    arrived = lax.all_to_all(outgoing, "docs", split_axis=0, concat_axis=0, tiled=True)
    arrived = arrived.reshape(arrivals, tile_rows, block_width)
    sender_blocks = all_blocks.reshape(peers, pairs)

    def sender_source(blocks):
        return send_order(blocks // BLK_OWN, capacity)[1]

    sender_sources = jax.vmap(sender_source)(sender_blocks)
    mine = lax.dynamic_slice_in_dim(sender_sources, lax.axis_index("docs") * capacity, capacity, 1)
    local_block = (jnp.take_along_axis(sender_blocks, mine, axis=1) % BLK_OWN).reshape(arrivals)
    tile_of = mine // slot_count
    sender_labels = all_labels[:, 0].reshape(peers, tiles_here, tile_rows)
    arrived_labels = jax.vmap(pick_tile)(sender_labels, tile_of).reshape(arrivals, tile_rows)
    cluster_hot = (
        arrived_labels[:, :, None] == jnp.arange(K, dtype=jnp.int32)[None, None, :]
    ).astype(jnp.bfloat16)
    contrib = jnp.einsum("rtk,rtb->rkb", cluster_hot, arrived, preferred_element_type=jnp.float32)
    block_hot = (local_block[:, None] == jnp.arange(BLK_OWN, dtype=jnp.int32)[None, :]).astype(
        jnp.float32
    )
    sums_own = jnp.einsum(
        "rc,rkb->kcb",
        block_hot,
        contrib,
        precision=lax.Precision.HIGHEST,
        preferred_element_type=jnp.float32,
    )
    sums_own = sums_own.reshape(K, BLK_OWN * block_width)
    sq_total = lax.psum(jnp.sum(sums_own * sums_own, axis=1), ("docs", "terms"))
    concepts_own = (sums_own * lax.rsqrt(sq_total + EPSILON)[:, None]).astype(jnp.bfloat16)
    gram_part = jnp.dot(concepts_own, concepts_own.T, preferred_element_type=jnp.float32)
    gram_matrix = lax.psum(gram_part, ("docs", "terms"))
    identity = jnp.eye(K, dtype=jnp.float32)
    factor = jnp.linalg.cholesky(gram_matrix + RIDGE_WEIGHT * identity)
    inverse = jax.scipy.linalg.cho_solve((factor, True), identity)
    concept_blocks = jnp.transpose(concepts_own.reshape(K, BLK_OWN, block_width), (1, 0, 2))
    wanted = concept_blocks[local_block]
    reply = lax.all_to_all(
        wanted.reshape(peers, capacity, K, block_width),
        "docs",
        split_axis=0,
        concat_axis=0,
        tiled=True,
    )
    fetched = reply.reshape(pairs, K, block_width)[own_target].reshape(
        tiles_here, slot_count, K, block_width
    )
    scores_part = jnp.einsum("isrb,iskb->irk", values, fetched, preferred_element_type=jnp.float32)
    scores_part = scores_part.reshape(doc_rows, K)
    col_width = K // lax.axis_size("terms")
    scores = lax.psum(scores_part, "terms")
    inverse_cols = lax.dynamic_slice_in_dim(
        inverse, lax.axis_index("terms") * col_width, col_width, 1
    )
    return jnp.dot(
        scores, inverse_cols, precision=lax.Precision.HIGHEST, preferred_element_type=jnp.float32
    )


def solution(mesh):
    in_specs = (P("docs", "terms", None, None), P("docs", "terms"), P("docs", None))
    out_specs = P("docs", "terms")
    return jax.shard_map(body, mesh=mesh, in_specs=in_specs, out_specs=out_specs, check_vma=False)
```

profile of v0, /device:TPU:2, one launch (start us, length us, event | category | flops | bytes accessed | tf_op | source)
XLA Modules:
  0.0 813.5 jit_solution(112224903261461516)
XLA Ops:
  11.2 12.0 %all-to-all-start = ((bf16[64,1,64,128]{3,2,1,0:T(8,128)(2,1)}), bf16[64,1,64,128]{3,2,1,0:T(8,128)(2,1)S(1)}, u32[]{:S(2)}, u32[]{:S(2)}) async-start(bf16[64,1,64,128]{3,2,1,0:T(8,128)(2,1)} %bitcast.7), calls=%async_computation | async-start | bytes 2097152 | tf_op jit(solution)/shard_map/all_to_all | solution.py:41
  23.3 67.7 %all-gather = s32[64,4,16]{2,1,0:T(4,128)S(1)} all-gather(s32[1,4,16]{2,1,0:T(4,128)} %bitcast.108), channel_id=1, replica_groups=mesh['docs'=64,'terms'=4] {'docs'}, dimensions={0}, use_global_device_ids=true | all-gather | bytes 16640 | tf_op jit(solution)/shard_map/all_gather | solution.py:35
  94.1 15.5 %scatter_custom_fusion.1 = s32[4096]{0:T(1024)S(1)} fusion(s32[4096]{0:T(1024)S(1)} %reshape.365, s32[4096]{0:T(1024)S(1)} %reshape.367, s32[]{:T(128)} %copy.156), kind=kCustom, calls=%fused_computation.147 | custom fusion | bytes 16388
  110.1 41.3 %all_gather.6 = s32[16384,1]{0,1:T(1,128)S(1)} all-gather(s32[256,1]{0,1:T(1,128)} %param.5), channel_id=1, replica_groups=mesh['docs'=64,'terms'=4] {'docs'}, dimensions={0}, use_global_device_ids=true | all-gather | bytes 66560 | tf_op jit(solution)/shard_map/all_gather | solution.py:36
  155.3 5.5 fusion.2
  160.8 26.4 %multiply_reduce_fusion = (f32[512]{0:T(512)S(1)}, f32[512,128,32]{1,2,0:T(8,128)}) fusion(s32[64]{0:T(128)S(1)} %get-tuple-element.14, f32[64,512,128]{2,1,0:T(8,128)S(1)} %fusion.2), kind=kOutput, calls=%fused_computation.12 | convolution fusion | flops 1614808576 | bytes 25168128 | tf_op jit(solution)/shard_map/rc,rkb->kcb/dot_general | solution.py:61
  187.2 77.1 %psum.21 = f32[512]{0:T(512)S(1)} all-reduce(f32[512]{0:T(512)S(1)} %get-tuple-element.45), channel_id=1, replica_groups=mesh['docs'=64,'terms'=4] {'docs','terms'}, use_global_device_ids=true, to_apply=%region_5.6 | all-reduce | flops 512 | bytes 4096 | tf_op jit(solution)/shard_map/psum | solution.py:69
  264.3 5.6 fusion.88
  269.9 3.5 copy.113
  273.4 7.7 gather_fusion.1
  281.1 9.2 %all-to-all-start.1 = ((bf16[64,1,512,128]{3,2,1,0:T(8,128)(2,1)}), bf16[64,1,512,128]{3,2,1,0:T(8,128)(2,1)}, u32[]{:S(2)}, u32[]{:S(2)}) async-start(bf16[64,1,512,128]{3,2,1,0:T(8,128)(2,1)} %bitcast.103), calls=%async_computation.1 | async-start | bytes 16777216 | tf_op jit(solution)/shard_map/all_to_all | solution.py:78
  290.4 6.9 fusion.6
  299.5 293.0 %all-reduce.6.cloned.1.call-done = f32[512,512]{0,1:T(8,128)} async-done(((f32[512,512]{0,1:T(8,128)}), f32[512,512]{0,1:T(8,128)}) %all-reduce.6.cloned.1.call-update) | async-done | bytes 1048592 | tf_op jit(solution)/shard_map/psum | solution.py:72
  595.7 11.7 %cholesky.104 = f32[128,128]{1,0:T(8,128)S(1)} custom-call(f32[128,128]{1,0:T(8,128)S(1)} %cholesky.266), custom_call_target="Cholesky" | custom-call | tf_op jit(solution)/shard_map/jit(cholesky)/cholesky | solution.py:74
  607.5 9.8 %custom-call.34 = f32[1,128,128]{1,2,0:T(8,128)S(1)} custom-call(f32[1,128,128]{2,1,0:T(8,128)S(1)} %get-tuple-element.38), custom_call_target="InvertDiagBlocksLowerTriangular" | custom-call | tf_op jit(solution)/shard_map/jit(cholesky)/cholesky | solution.py:74
  618.0 11.7 %cholesky.217 = f32[128,128]{1,0:T(8,128)S(1)} custom-call(f32[128,128]{1,0:T(8,128)S(1)} %cholesky.270), custom_call_target="Cholesky" | custom-call | tf_op jit(solution)/shard_map/jit(cholesky)/cholesky | solution.py:74
  629.8 10.0 %custom-call.35 = f32[1,128,128]{1,2,0:T(8,128)S(1)} custom-call(f32[1,128,128]{2,1,0:T(8,128)S(1)} %get-tuple-element.35), custom_call_target="InvertDiagBlocksLowerTriangular" | custom-call | tf_op jit(solution)/shard_map/jit(cholesky)/cholesky | solution.py:74
  640.4 11.7 %cholesky.238 = f32[128,128]{1,0:T(8,128)S(1)} custom-call(f32[128,128]{1,0:T(8,128)S(1)} %cholesky.275), custom_call_target="Cholesky" | custom-call | tf_op jit(solution)/shard_map/jit(cholesky)/cholesky | solution.py:74
  652.2 9.8 %custom-call.36 = f32[1,128,128]{1,2,0:T(8,128)S(1)} custom-call(f32[1,128,128]{2,1,0:T(8,128)S(1)} %get-tuple-element.32), custom_call_target="InvertDiagBlocksLowerTriangular" | custom-call | tf_op jit(solution)/shard_map/jit(cholesky)/cholesky | solution.py:74
  662.6 11.7 %cholesky.255 = f32[128,128]{1,0:T(8,128)S(1)} custom-call(f32[128,128]{1,0:T(8,128)S(1)} %convolution_subtract_fusion.8), custom_call_target="Cholesky" | custom-call | tf_op jit(solution)/shard_map/jit(cholesky)/cholesky | solution.py:74
  679.9 10.5 %while.1 = (s32[]{:T(128)}, f32[512,512]{1,0:T(8,128)S(1)}, s32[4,2]{0,1:T(2,128)S(1)}, f32[4,128,128]{2,1,0:T(8,128)}, s32[]{:T(128)}) while((s32[]{:T(128)}, f32[512,512]{1,0:T(8,128)S(1)}, s32[4,2]{0,1:T(2,128)S(1)}, f32[4,128,128]{2,1,0:T(8,128)}, s32[]{:T(128)}) %tuple.35), condition=%wide.while_cond, body=%wide.while_body.sunk | while | flops 2 | bytes 132705 | solution.py:75
  680.6 2.0 bitcast_dynamic-update-slice_fusion.2
  683.2 2.0 bitcast_dynamic-update-slice_fusion.2
  685.8 2.0 bitcast_dynamic-update-slice_fusion.2
  688.5 2.0 bitcast_dynamic-update-slice_fusion.2
  690.4 40.1 %custom-call.37 = f32[4,128,128]{1,2,0:T(8,128)S(1)} custom-call(f32[4,128,128]{2,1,0:T(8,128)} %get-tuple-element.12), custom_call_target="InvertDiagBlocksLowerTriangular" | custom-call | tf_op jit(solution)/shard_map/jit(_cho_solve)/triangular_solve | solution.py:75
  733.6 1.9 convolution_subtract_fusion.2
  736.0 2.4 convolution_subtract_fusion.5
  741.2 8.9 %gather_fusion.2 = bf16[64,512,128]{2,1,0:T(8,128)(2,1)} fusion(bf16[64,512,128]{2,1,0:T(8,128)(2,1)} %bitcast.15, s32[1024]{0:T(1024)S(1)} %pad_clamp_fusion), kind=kCustom, calls=%fused_computation.2 | custom fusion | bytes 16777472 | tf_op jit(solution)/shard_map/gather | solution.py:85
  750.1 6.8 fusion.93
  759.3 44.3 %all-reduce.4.cloned.1.call-done = f32[256,512]{1,0:T(8,128)} async-done(((f32[256,512]{1,0:T(8,128)}), f32[256,512]{1,0:T(8,128)}) %all-reduce.4.cloned.1.call-update) | async-done | bytes 524304 | tf_op jit(solution)/shard_map/psum | solution.py:91
  803.6 2.3 fusion.31
  (101 shorter events, 33.1 us)
Async XLA Ops:
  7.4 2.2 copy-start
  11.2 144.1 %all-to-all-start = ((bf16[64,1,64,128]{3,2,1,0:T(8,128)(2,1)}), bf16[64,1,64,128]{3,2,1,0:T(8,128)(2,1)S(1)}, u32[]{:S(2)}, u32[]{:S(2)}) async-start(bf16[64,1,64,128]{3,2,1,0:T(8,128)(2,1)} %bitcast.7), calls=%async_computation | async-start | bytes 2097152 | tf_op jit(solution)/shard_map/all_to_all | solution.py:41
  281.1 460.0 %all-to-all-start.1 = ((bf16[64,1,512,128]{3,2,1,0:T(8,128)(2,1)}), bf16[64,1,512,128]{3,2,1,0:T(8,128)(2,1)}, u32[]{:S(2)}, u32[]{:S(2)}) async-start(bf16[64,1,512,128]{3,2,1,0:T(8,128)(2,1)} %bitcast.103), calls=%async_computation.1 | async-start | bytes 16777216 | tf_op jit(solution)/shard_map/all_to_all | solution.py:78
  290.4 302.2 %all-reduce.6.cloned.1.call-start = ((), (), s32[]{:S(2)}) async-start(), calls=%async_computation.3 | async-start | bytes 2097152 | tf_op jit(solution)/shard_map/psum | solution.py:72
  297.3 506.3 %all-reduce.4.cloned.1.call-start = ((), (), s32[]{:S(2)}) async-start(), calls=%async_computation.2 | async-start | bytes 1048576 | tf_op jit(solution)/shard_map/psum | solution.py:91
Sparse Core Ops, SparseCore 0:
  297.4 295.0 all-reduce.5
Sparse Core Ops, SparseCore 1:
  757.0 46.6 all-reduce.3
where the time goes:
time: 821 us; the launch traced here: 813 us
  waiting for transfers between devices  337 us (41%)
  blocking collectives  186 us (23%)
  other arithmetic  135 us (16%)
  matrix products  62.6 us (8%)
  local copies, waits for them, and re-layouts  52.6 us (6%)
  starting transfers between devices  21.5 us (3%)
  between operations  17.9 us (2%)
    psum x1, waiting for transfers between devices, body(): gram_matrix = lax.psum(gram_part, ('docs', 'terms'))  293 us
    another operation x15, other arithmetic, body(): factor = jnp.linalg.cholesky(gram_matrix + RIDGE_WEIGHT * identity)  79.6 us
    psum x1, blocking collectives, body(): sq_total = lax.psum(jnp.sum(sums_own * sums_own, axis=1), ('docs', 'terms'))  77.1 us
    all_gather x1, blocking collectives, body(): lax.all_gather(block_ids, 'docs', axis=0, tiled=True)  67.7 us
    psum x1, waiting for transfers between devices, body(): scores = lax.psum(scores_part, 'terms')  44.3 us
    all_gather x1, blocking collectives, body(): lax.all_gather(assignment, 'docs', axis=0, tiled=True)  41.3 us
    another operation x3, other arithmetic, body(): inverse = jax.scipy.linalg.cho_solve((factor, True), identity)  40.3 us
    dot_general x1, matrix products, body(): jnp.einsum('rc,rkb->kcb', block_hot, contrib, precision=lax.Precision.HIG...  26.4 us
  transfers between devices with their start and end apart: 4, of which 2 were waited for; matrix products, arithmetic and copies ran while one was open for 22% of the time, Pallas kernels for 0%

commit v1 on v0

--- a/solution.py
+++ b/solution.py
@@ -33,7 +33,9 @@
     doc_rows = tiles_here * tile_rows
     all_blocks, all_labels = (
         lax.all_gather(block_ids, "docs", axis=0, tiled=True),
-        lax.all_gather(assignment, "docs", axis=0, tiled=True),
+        jnp.concatenate(
+            lax.all_to_all(jnp.stack([assignment] * lax.axis_size("docs")), "docs", 0, 0), axis=0
+        ),
     )
     own_target, own_source = send_order((block_ids // BLK_OWN).reshape(pairs), capacity)
     flat_values = values.reshape(pairs, tile_rows, block_width)

time: 821 us -> 790 us (0.962)
  blocking collectives: 186 us -> 145 us
    all_gather x1 -> x0, blocking collectives: 41.3 us -> none  [body(): lax.all_gather(assignment, 'docs', axis=0, tiled=True)]
    all_to_all x0 -> x1, starting transfers between devices: none -> 12 us  [body(): lax.all_to_all(jnp.stack([assignment] * lax.axis_size('docs')), 'docs', 0...]
  transfers between devices with their start and end apart: 4 -> 5, of which waited for: 2 -> 3; matrix products, arithmetic and copies ran while one was open for 22% -> 23% of each run, Pallas kernels for 0% -> 0%
where the time goes in v1:
time: 790 us; the launch traced here: 782 us
  waiting for transfers between devices  343 us (43%)
  blocking collectives  145 us (18%)
  other arithmetic  135 us (17%)
  matrix products  62.6 us (8%)
  local copies, waits for them, and re-layouts  53 us (7%)
  starting transfers between devices  26.1 us (3%)
  between operations  18 us (2%)
    psum x1, waiting for transfers between devices, body(): gram_matrix = lax.psum(gram_part, ('docs', 'terms'))  294 us
    another operation x15, other arithmetic, body(): factor = jnp.linalg.cholesky(gram_matrix + RIDGE_WEIGHT * identity)  79.5 us
    psum x1, blocking collectives, body(): sq_total = lax.psum(jnp.sum(sums_own * sums_own, axis=1), ('docs', 'terms'))  77.2 us
    all_gather x1, blocking collectives, body(): lax.all_gather(block_ids, 'docs', axis=0, tiled=True)  67.7 us
    psum x1, waiting for transfers between devices, body(): scores = lax.psum(scores_part, 'terms')  44.3 us
    another operation x3, other arithmetic, body(): inverse = jax.scipy.linalg.cho_solve((factor, True), identity)  40.3 us
    dot_general x1, matrix products, body(): jnp.einsum('rc,rkb->kcb', block_hot, contrib, precision=lax.Precision.HIG...  26.4 us
    unnamed x10, local copies, waits for them, and re-layouts  16 us
  transfers between devices with their start and end apart: 5, of which 3 were waited for; matrix products, arithmetic and copies ran while one was open for 23% of the time, Pallas kernels for 0%

profile of v1, /device:TPU:2, one launch (start us, length us, event | category | flops | bytes accessed | tf_op | source)
XLA Modules:
  0.0 782.1 jit_solution(15097769837618460364)
XLA Ops:
  8.8 12.0 %all-to-all-start = ((s32[64,256,1]{1,2,0:T(1,128)}), s32[64,256,1]{1,2,0:T(1,128)S(1)}, u32[]{:S(2)}, u32[]{:S(2)}) async-start(s32[64,256,1]{1,2,0:T(1,128)} %stack.2), calls=%async_computation | async-start | bytes 131072 | tf_op jit(solution)/shard_map/all_to_all | solution.py:37
  24.6 5.1 all-to-all-done
  29.7 5.5 all-to-all-start.1
  35.2 67.7 %all-gather = s32[64,4,16]{2,1,0:T(4,128)S(1)} all-gather(s32[1,4,16]{2,1,0:T(4,128)} %bitcast.108), channel_id=1, replica_groups=mesh['docs'=64,'terms'=4] {'docs'}, dimensions={0}, use_global_device_ids=true | all-gather | bytes 16640 | tf_op jit(solution)/shard_map/all_gather | solution.py:35
  106.1 15.5 %scatter_custom_fusion.1 = s32[4096]{0:T(1024)S(1)} fusion(s32[4096]{0:T(1024)S(1)} %reshape.368, s32[4096]{0:T(1024)S(1)} %reshape.370, s32[]{:T(128)} %copy.156), kind=kCustom, calls=%fused_computation.147 | custom fusion | bytes 16388
  124.7 5.5 fusion.2
  130.2 26.4 %multiply_reduce_fusion = (f32[512]{0:T(512)S(1)}, f32[512,128,32]{1,2,0:T(8,128)}) fusion(s32[64]{0:T(128)S(1)} %get-tuple-element.14, f32[64,512,128]{2,1,0:T(8,128)S(1)} %fusion.2), kind=kOutput, calls=%fused_computation.12 | convolution fusion | flops 1614808576 | bytes 25168128 | tf_op jit(solution)/shard_map/rc,rkb->kcb/dot_general | solution.py:63
  156.6 77.2 %psum.21 = f32[512]{0:T(512)S(1)} all-reduce(f32[512]{0:T(512)S(1)} %get-tuple-element.45), channel_id=1, replica_groups=mesh['docs'=64,'terms'=4] {'docs','terms'}, use_global_device_ids=true, to_apply=%region_5.6 | all-reduce | flops 512 | bytes 4096 | tf_op jit(solution)/shard_map/psum | solution.py:71
  233.8 5.6 fusion.88
  239.4 3.5 copy.113
  242.9 7.7 gather_fusion.1
  250.6 8.3 %all-to-all-start.2 = ((bf16[64,1,512,128]{3,2,1,0:T(8,128)(2,1)}), bf16[64,1,512,128]{3,2,1,0:T(8,128)(2,1)}, u32[]{:S(2)}, u32[]{:S(2)}) async-start(bf16[64,1,512,128]{3,2,1,0:T(8,128)(2,1)} %bitcast.103), calls=%async_computation.2 | async-start | bytes 16777216 | tf_op jit(solution)/shard_map/all_to_all | solution.py:80
  258.9 6.9 fusion.6
  268.0 293.6 %all-reduce.6.cloned.1.call-done = f32[512,512]{0,1:T(8,128)} async-done(((f32[512,512]{0,1:T(8,128)}), f32[512,512]{0,1:T(8,128)}) %all-reduce.6.cloned.1.call-update) | async-done | bytes 1048592 | tf_op jit(solution)/shard_map/psum | solution.py:74
  564.7 11.7 %cholesky.104 = f32[128,128]{1,0:T(8,128)S(1)} custom-call(f32[128,128]{1,0:T(8,128)S(1)} %cholesky.266), custom_call_target="Cholesky" | custom-call | tf_op jit(solution)/shard_map/jit(cholesky)/cholesky | solution.py:76
  576.6 9.8 %custom-call.34 = f32[1,128,128]{1,2,0:T(8,128)S(1)} custom-call(f32[1,128,128]{2,1,0:T(8,128)S(1)} %get-tuple-element.38), custom_call_target="InvertDiagBlocksLowerTriangular" | custom-call | tf_op jit(solution)/shard_map/jit(cholesky)/cholesky | solution.py:76
  587.1 11.7 %cholesky.217 = f32[128,128]{1,0:T(8,128)S(1)} custom-call(f32[128,128]{1,0:T(8,128)S(1)} %cholesky.270), custom_call_target="Cholesky" | custom-call | tf_op jit(solution)/shard_map/jit(cholesky)/cholesky | solution.py:76
  598.8 10.0 %custom-call.35 = f32[1,128,128]{1,2,0:T(8,128)S(1)} custom-call(f32[1,128,128]{2,1,0:T(8,128)S(1)} %get-tuple-element.35), custom_call_target="InvertDiagBlocksLowerTriangular" | custom-call | tf_op jit(solution)/shard_map/jit(cholesky)/cholesky | solution.py:76
  609.5 11.7 %cholesky.238 = f32[128,128]{1,0:T(8,128)S(1)} custom-call(f32[128,128]{1,0:T(8,128)S(1)} %cholesky.275), custom_call_target="Cholesky" | custom-call | tf_op jit(solution)/shard_map/jit(cholesky)/cholesky | solution.py:76
  621.3 9.8 %custom-call.36 = f32[1,128,128]{1,2,0:T(8,128)S(1)} custom-call(f32[1,128,128]{2,1,0:T(8,128)S(1)} %get-tuple-element.32), custom_call_target="InvertDiagBlocksLowerTriangular" | custom-call | tf_op jit(solution)/shard_map/jit(cholesky)/cholesky | solution.py:76
  631.7 11.7 %cholesky.255 = f32[128,128]{1,0:T(8,128)S(1)} custom-call(f32[128,128]{1,0:T(8,128)S(1)} %convolution_subtract_fusion.8), custom_call_target="Cholesky" | custom-call | tf_op jit(solution)/shard_map/jit(cholesky)/cholesky | solution.py:76
  649.0 10.1 %while.1 = (s32[]{:T(128)}, f32[512,512]{1,0:T(8,128)S(1)}, s32[4,2]{0,1:T(2,128)S(1)}, f32[4,128,128]{2,1,0:T(8,128)}, s32[]{:T(128)}) while((s32[]{:T(128)}, f32[512,512]{1,0:T(8,128)S(1)}, s32[4,2]{0,1:T(2,128)S(1)}, f32[4,128,128]{2,1,0:T(8,128)}, s32[]{:T(128)}) %tuple.35), condition=%wide.while_cond, body=%wide.while_body.sunk | while | flops 2 | bytes 132705 | solution.py:77
  649.6 1.9 bitcast_dynamic-update-slice_fusion.2
  652.1 1.9 bitcast_dynamic-update-slice_fusion.2
  654.7 1.9 bitcast_dynamic-update-slice_fusion.2
  659.1 40.1 %custom-call.37 = f32[4,128,128]{1,2,0:T(8,128)S(1)} custom-call(f32[4,128,128]{2,1,0:T(8,128)} %get-tuple-element.12), custom_call_target="InvertDiagBlocksLowerTriangular" | custom-call | tf_op jit(solution)/shard_map/jit(_cho_solve)/triangular_solve | solution.py:77
  702.3 1.9 convolution_subtract_fusion.2
  704.7 2.4 convolution_subtract_fusion.5
  709.8 8.9 %gather_fusion.2 = bf16[64,512,128]{2,1,0:T(8,128)(2,1)} fusion(bf16[64,512,128]{2,1,0:T(8,128)(2,1)} %bitcast.16, s32[1024]{0:T(1024)S(1)} %pad_clamp_fusion), kind=kCustom, calls=%fused_computation.2 | custom fusion | bytes 16777472 | tf_op jit(solution)/shard_map/gather | solution.py:87
  718.7 6.8 fusion.93
  727.9 44.3 %all-reduce.4.cloned.1.call-done = f32[256,512]{1,0:T(8,128)} async-done(((f32[256,512]{1,0:T(8,128)}), f32[256,512]{1,0:T(8,128)}) %all-reduce.4.cloned.1.call-update) | async-done | bytes 524304 | tf_op jit(solution)/shard_map/psum | solution.py:93
  772.3 2.3 fusion.31
  (102 shorter events, 34.7 us)
Async XLA Ops:
  7.4 15.5 %copy-start = (bf16[4,16,64,128]{3,2,1,0:T(8,128)(2,1)S(1)}, bf16[4,16,64,128]{3,2,1,0:T(8,128)(2,1)}, u32[]{:S(2)}) copy-start(bf16[4,16,64,128]{3,2,1,0:T(8,128)(2,1)} %param.3) | copy-start | bytes 3145732
  8.8 20.9 %all-to-all-start = ((s32[64,256,1]{1,2,0:T(1,128)}), s32[64,256,1]{1,2,0:T(1,128)S(1)}, u32[]{:S(2)}, u32[]{:S(2)}) async-start(s32[64,256,1]{1,2,0:T(1,128)} %stack.2), calls=%async_computation | async-start | bytes 131072 | tf_op jit(solution)/shard_map/all_to_all | solution.py:37
  29.7 95.0 %all-to-all-start.1 = ((bf16[64,1,64,128]{3,2,1,0:T(8,128)(2,1)}), bf16[64,1,64,128]{3,2,1,0:T(8,128)(2,1)S(1)}, u32[]{:S(2)}, u32[]{:S(2)}) async-start(bf16[64,1,64,128]{3,2,1,0:T(8,128)(2,1)} %bitcast.8), calls=%async_computation.1 | async-start | bytes 2097152 | tf_op jit(solution)/shard_map/all_to_all | solution.py:43
  250.6 459.2 %all-to-all-start.2 = ((bf16[64,1,512,128]{3,2,1,0:T(8,128)(2,1)}), bf16[64,1,512,128]{3,2,1,0:T(8,128)(2,1)}, u32[]{:S(2)}, u32[]{:S(2)}) async-start(bf16[64,1,512,128]{3,2,1,0:T(8,128)(2,1)} %bitcast.103), calls=%async_computation.2 | async-start | bytes 16777216 | tf_op jit(solution)/shard_map/all_to_all | solution.py:80
  258.9 302.7 %all-reduce.6.cloned.1.call-start = ((), (), s32[]{:S(2)}) async-start(), calls=%async_computation.4 | async-start | bytes 2097152 | tf_op jit(solution)/shard_map/psum | solution.py:74
  265.8 506.4 %all-reduce.4.cloned.1.call-start = ((), (), s32[]{:S(2)}) async-start(), calls=%async_computation.3 | async-start | bytes 1048576 | tf_op jit(solution)/shard_map/psum | solution.py:93
Sparse Core Ops, SparseCore 0:
  266.0 295.5 all-reduce.5
Sparse Core Ops, SparseCore 1:
  725.6 46.6 all-reduce.3
